TPU v7x, 256 devices: a whole 4x4x8 slice. The times are simulated.
256 devices in a mesh: seq: 8 (over z_hi, x), exp: 32 (over z_lo, y, core).
Axes of the slice: x: 4, y: 4, z: 8 (z_hi: 2, z_lo: 4; z = z_hi * 4 + z_lo), core: 2. Of those that a mesh axis runs over, the one named last changes fastest.
Arguments:
- tokens: bfloat16 [8192, 1664], P('seq'), may hold values from -6 to 6
- out_grad: bfloat16 [8192, 1664], P('seq'), may hold values from -6 to 6
- slot_params: bfloat16 [1024, 1664], P('exp'), may hold values from -6 to 6
- first_mixing: float32 [64, 4, 4, 4], P('exp'), may hold values from -3 to 3
- first_blocks: bfloat16 [64, 4, 416, 2048], P('exp', None, None, 'seq'), may hold values from -0.15625 to 0.15625
- second_mixing: float32 [64, 4, 4, 4], P('exp'), may hold values from -3 to 3
- second_blocks: bfloat16 [64, 4, 2048, 416], P('exp', None, 'seq'), may hold values from -0.0625 to 0.0625
Outputs:
- grad_tokens: float32 [8192, 1664], P(('seq', 'exp'))
- grad_slots: float32 [1024, 1664], P('exp')
- grad_first_mixing: float32 [64, 4, 4, 4], P('exp')
- grad_first_blocks: bfloat16 [64, 4, 416, 2048], P('exp', None, None, 'seq')
- grad_second_mixing: float32 [64, 4, 4, 4], P('exp')
- grad_second_blocks: bfloat16 [64, 4, 2048, 416], P('exp', None, 'seq')
All inputs are finite; a program needn't handle non-finite values.
Results may differ from a plain program's by a relative error of at most 0.04.
Values may be sent and summed in bfloat16 or wider, within the bound.
No kernel may reach another device: no remote copies, remote signals or barrier semaphores. Data moves between devices by JAX's collectives and lax.ppermute only.
A program may use at most 128 MiB of HBM per device.

v0:
```python
import jax
import jax.numpy as jnp
from jax import lax
from jax.sharding import PartitionSpec as P

logit_gain = 64.0
norm_eps = 1e-06
gelu_coef = 0.7978845608028654
cubic_coef = 0.044715


def gelu_pair(preact):
    inner_arg = gelu_coef * (preact + cubic_coef * preact * preact * preact)
    tangent = jnp.tanh(inner_arg)
    output = 0.5 * preact * (1.0 + tangent)
    slopes = 0.5 * (1.0 + tangent) + 0.5 * preact * (1.0 - tangent * tangent) * gelu_coef * (
        1.0 + 3.0 * cubic_coef * preact * preact
    )
    return (output, slopes)


def mix_blocks(blocks, mixing):
    return jnp.einsum("sak,iab->sbik", blocks.astype(jnp.float32), mixing)


def expert_forward(slot_in, first_mixing, first_blocks, second_mixing, second_blocks):
    slots_here, model_width = slot_in.shape
    factors = first_mixing.shape[0]
    inner_width = model_width // factors
    hidden_block = first_blocks.shape[2]
    first_flat = (
        mix_blocks(slot_in.reshape(slots_here, factors, inner_width), first_mixing)
        .astype(jnp.bfloat16)
        .reshape(slots_here * factors, factors * inner_width)
    )
    preact = jnp.dot(
        first_flat,
        first_blocks.reshape(factors * inner_width, hidden_block),
        preferred_element_type=jnp.float32,
    ).reshape(slots_here, factors, hidden_block)
    activated, slopes = gelu_pair(preact)
    hidden = activated.astype(jnp.bfloat16)
    second_flat = (
        mix_blocks(hidden, second_mixing)
        .astype(jnp.bfloat16)
        .reshape(slots_here * factors, factors * hidden_block)
    )
    slot_out = jnp.dot(
        second_flat,
        second_blocks.reshape(factors * hidden_block, inner_width),
        preferred_element_type=jnp.float32,
    ).reshape(slots_here, model_width)
    return (slot_out, first_flat, hidden, slopes, second_flat)


def expert_backward(
    slot_in,
    grad_out,
    first_flat,
    hidden,
    slopes,
    second_flat,
    first_mixing,
    first_blocks,
    second_mixing,
    second_blocks,
):
    slots_here, model_width = slot_in.shape
    factors = first_mixing.shape[0]
    inner_width = model_width // factors
    hidden_block = first_blocks.shape[2]
    first_matrix = first_blocks.reshape(factors * inner_width, hidden_block)
    second_matrix = second_blocks.reshape(factors * hidden_block, inner_width)
    grad_rows = grad_out.reshape(slots_here * factors, inner_width)
    grad_second_in = jnp.dot(
        grad_rows, second_matrix.T, preferred_element_type=jnp.float32
    ).reshape(slots_here, factors, factors, hidden_block)
    grad_second_blocks = (
        jnp.dot(second_flat.T, grad_rows, preferred_element_type=jnp.float32)
        .astype(jnp.bfloat16)
        .reshape(factors, hidden_block, inner_width)
    )
    grad_second_mixing = jnp.einsum("sak,sbik->iab", hidden.astype(jnp.float32), grad_second_in)
    grad_hidden = jnp.einsum("iab,sbik->sak", second_mixing, grad_second_in)
    grad_preact = (
        (grad_hidden * slopes).astype(jnp.bfloat16).reshape(slots_here * factors, hidden_block)
    )
    grad_first_in = jnp.dot(
        grad_preact, first_matrix.T, preferred_element_type=jnp.float32
    ).reshape(slots_here, factors, factors, inner_width)
    grad_first_blocks = (
        jnp.dot(first_flat.T, grad_preact, preferred_element_type=jnp.float32)
        .astype(jnp.bfloat16)
        .reshape(factors, inner_width, hidden_block)
    )
    slot_split = slot_in.reshape(slots_here, factors, inner_width).astype(jnp.float32)
    grad_first_mixing = jnp.einsum("sad,sbid->iab", slot_split, grad_first_in)
    grad_slot = jnp.einsum("iab,sbid->sad", first_mixing, grad_first_in).reshape(
        slots_here, model_width
    )
    return (grad_slot, grad_first_mixing, grad_first_blocks, grad_second_mixing, grad_second_blocks)


def token_total(partial_sums):
    return lax.psum(partial_sums, "exp")


def slot_total(first_part, second_part):
    return lax.psum((first_part, second_part), "seq")


def unit_grad(unit_rows, unit_grad_rows, norms):
    return (
        unit_grad_rows - unit_rows * jnp.sum(unit_rows * unit_grad_rows, axis=1, keepdims=True)
    ) / norms


def local(tokens, out_grad, slot_params, first_mixing, first_blocks, second_mixing, second_blocks):
    token_values = tokens.astype(jnp.float32)
    token_norm = jnp.sqrt(jnp.sum(token_values * token_values, axis=1, keepdims=True) + norm_eps)
    token_unit = token_values / token_norm
    token_unit_b = token_unit.astype(jnp.bfloat16)
    slot_values = slot_params.astype(jnp.float32)
    slot_norm = jnp.sqrt(jnp.sum(slot_values * slot_values, axis=1, keepdims=True) + norm_eps)
    slot_unit = slot_values / slot_norm
    slot_unit_b = slot_unit.astype(jnp.bfloat16)
    logits = logit_gain * jnp.einsum(
        "sd,td->st", slot_unit_b, token_unit_b, preferred_element_type=jnp.float32
    )
    weights = jnp.exp(logits)
    input_part = jnp.dot(weights.astype(jnp.bfloat16), tokens, preferred_element_type=jnp.float32)
    combine_total = token_total(jnp.sum(weights, axis=0))
    input_sum, dispatch_total = slot_total(input_part, jnp.sum(weights, axis=1))
    slot_inputs = input_sum / dispatch_total[:, None]
    slot_inputs_b = slot_inputs.astype(jnp.bfloat16)
    dispatch = weights / dispatch_total[:, None]
    combine = weights / combine_total[None, :]
    grad_out_part = jnp.dot(
        combine.astype(jnp.bfloat16), out_grad, preferred_element_type=jnp.float32
    )
    experts_here = first_mixing.shape[0]
    model_width = tokens.shape[1]
    slots_each = slot_inputs_b.shape[0] // experts_here
    grouped = slot_inputs_b.reshape(experts_here, slots_each, model_width)
    slot_out_part, first_flat, hidden, slopes, second_flat = jax.vmap(expert_forward)(
        grouped, first_mixing, first_blocks, second_mixing, second_blocks
    )
    slot_out_sum, slot_grad_sum = slot_total(
        slot_out_part.reshape(experts_here * slots_each, model_width), grad_out_part
    )
    slot_out_b = slot_out_sum.astype(jnp.bfloat16)
    slot_grad_b = slot_grad_sum.astype(jnp.bfloat16)
    combine_grad = jnp.einsum("sd,td->st", slot_out_b, out_grad, preferred_element_type=jnp.float32)
    combine_dot = token_total(jnp.sum(combine * combine_grad, axis=0))
    expert_results = jax.vmap(expert_backward)(
        grouped,
        slot_grad_b.reshape(experts_here, slots_each, model_width),
        first_flat,
        hidden,
        slopes,
        second_flat,
        first_mixing,
        first_blocks,
        second_mixing,
        second_blocks,
    )
    input_grad_part, first_mix_part, first_blocks_grad, second_mix_part, second_blocks_grad = (
        expert_results
    )
    input_grad, mixing_grads = slot_total(
        input_grad_part.reshape(experts_here * slots_each, model_width),
        jnp.stack([first_mix_part, second_mix_part]),
    )
    input_grad_b = input_grad.astype(jnp.bfloat16)
    dispatch_dot = jnp.sum(slot_inputs * input_grad, axis=1)
    dispatch_grad = jnp.einsum(
        "sd,td->st", input_grad_b, tokens, preferred_element_type=jnp.float32
    )
    logit_grad = combine * (combine_grad - combine_dot[None, :]) + dispatch * (
        dispatch_grad - dispatch_dot[:, None]
    )
    logit_grad_b = (logit_gain * logit_grad).astype(jnp.bfloat16)
    slot_unit_grad = lax.psum(
        jnp.dot(logit_grad_b, token_unit_b, preferred_element_type=jnp.float32), "seq"
    )
    grad_slots = unit_grad(slot_unit, slot_unit_grad, slot_norm)
    row_count = tokens.shape[0] // lax.axis_size("exp")
    grad_all, out_all, unit_all = (
        lax.all_gather(input_grad_b, "exp", axis=0, tiled=True),
        lax.all_gather(slot_out_b, "exp", axis=0, tiled=True),
        lax.all_gather(slot_unit_b, "exp", axis=0, tiled=True),
    )
    dispatch_all, dot_all = (
        lax.all_gather(dispatch_total, "exp", axis=0, tiled=True),
        lax.all_gather(dispatch_dot, "exp", axis=0, tiled=True),
    )
    first_row = lax.axis_index("exp") * row_count
    own_tokens = lax.dynamic_slice_in_dim(tokens, first_row, row_count, 0)
    own_grad = lax.dynamic_slice_in_dim(out_grad, first_row, row_count, 0)
    own_unit = lax.dynamic_slice_in_dim(token_unit, first_row, row_count, 0)
    own_unit_b = lax.dynamic_slice_in_dim(token_unit_b, first_row, row_count, 0)
    own_norm = lax.dynamic_slice_in_dim(token_norm, first_row, row_count, 0)
    own_total = lax.dynamic_slice_in_dim(combine_total, first_row, row_count, 0)
    own_dot = lax.dynamic_slice_in_dim(combine_dot, first_row, row_count, 0)
    own_weights = jnp.exp(
        logit_gain * jnp.dot(own_unit_b, unit_all.T, preferred_element_type=jnp.float32)
    )
    own_dispatch = own_weights / dispatch_all[None, :]
    own_combine = own_weights / own_total[:, None]
    own_combine_grad = jnp.dot(own_grad, out_all.T, preferred_element_type=jnp.float32)
    own_dispatch_grad = jnp.dot(own_tokens, grad_all.T, preferred_element_type=jnp.float32)
    own_logit = own_combine * (own_combine_grad - own_dot[:, None]) + own_dispatch * (
        own_dispatch_grad - dot_all[None, :]
    )
    own_logit_b = (logit_gain * own_logit).astype(jnp.bfloat16)
    direct = jnp.dot(
        own_dispatch.astype(jnp.bfloat16), grad_all, preferred_element_type=jnp.float32
    )
    through = jnp.dot(own_logit_b, unit_all, preferred_element_type=jnp.float32)
    grad_tokens = direct + unit_grad(own_unit, through, own_norm)
    return (
        grad_tokens,
        grad_slots,
        mixing_grads[0],
        first_blocks_grad,
        mixing_grads[1],
        second_blocks_grad,
    )


def solution(mesh):
    placed = (
        P("seq", None),
        P("seq", None),
        P("exp", None),
        P("exp", None, None, None),
        P("exp", None, None, "seq"),
        P("exp", None, None, None),
        P("exp", None, "seq", None),
    )
    return jax.shard_map(
        local,
        mesh=mesh,
        in_specs=placed,
        out_specs=(
            P(("seq", "exp"), None),
            P("exp", None),
            P("exp", None, None, None),
            P("exp", None, None, "seq"),
            P("exp", None, None, None),
            P("exp", None, "seq", None),
        ),
        check_vma=False,
    )
```

profile of v0, /device:TPU:1, one launch (start us, length us, event | category | flops | bytes accessed | tf_op | source)
XLA Modules:
  0.0 651.7 jit_solution(12688127571988477652)
XLA Ops:
  8.1 2.9 fusion
  11.2 5.0 convert_divide_fusion
  16.3 0.6 copy-done.16
  16.9 0.7 fusion.55
  17.6 3.9 fusion.57
  21.6 1.4 fusion.39
  23.0 71.5 %psum.64 = f32[1024]{0:T(1024)S(1)} all-reduce(f32[1024]{0:T(1024)S(1)} %get-tuple-element.19), channel_id=1, replica_groups=mesh['seq'=8,'exp'=32] {'exp'}, use_global_device_ids=true, to_apply=%region_5.0 | all-reduce | flops 1024 | bytes 8192 | tf_op jit(solution)/shard_map/psum | solution.py:105
  94.5 0.6 copy-done.10
  95.1 1.4 fusion.41
  96.5 50.3 %all-reduce.16 = (bf16[32,1664]{1,0:T(8,128)(2,1)}, f32[32]{0:T(128)}) all-reduce(f32[32,1664]{1,0:T(8,128)} %fusion.41, f32[32]{0:T(128)} %get-tuple-element.18), channel_id=1, replica_groups=mesh['seq'=8,'exp'=32] {'seq'}, use_global_device_ids=true, to_apply=%region_6.0 | all-reduce | flops 53280 | bytes 319744 | tf_op jit(solution)/shard_map/psum | solution.py:109
  146.8 1.7 reshape_reshape.7
  148.5 1.7 copy.55
  150.2 1.2 copy-done.3
  151.4 1.1 fusion.66
  152.5 1.8 reshape.84
  154.4 1.4 copy.34
  155.8 0.7 copy.38
  156.6 1.3 dynamic-slice.4
  158.5 0.6 broadcast.43.clone.1
  159.1 1.4 dynamic-update-slice
  160.4 1.7 fusion.46
  162.1 1.7 reshape.107
  163.8 1.4 fusion.1
  165.2 1.1 copy.25
  166.3 2.3 reshape.85
  168.6 2.7 fusion.67
  171.2 1.6 reshape.87
  172.8 2.0 fusion.2
  174.8 1.9 convolution_bitcast_fusion.3
  176.7 2.0 fusion.15
  178.7 1.5 reshape.88
  180.2 2.9 fusion.68
  183.0 2.5 reshape.89
  185.6 2.2 convolution_bitcast_fusion.2
  187.8 0.8 copy.30
  188.6 1.4 copy.32
  190.1 1.8 copy.28
  191.8 1.8 reshape.91
  193.6 2.9 fusion.69
  196.5 1.8 reshape.92
  198.3 2.2 convolution_bitcast_fusion
  200.4 1.9 reshape.90
  202.4 1.3 pad_maximum_fusion
  203.7 46.9 %all-reduce.17 = (bf16[32,1664]{1,0:T(8,128)(2,1)}, f32[2,2,4,4,4]{4,3,2,1,0:T(4,128)}) all-reduce(f32[32,1664]{1,0:T(8,128)} %reshape.92, f32[2,2,4,4,4]{4,3,2,1,0:T(4,128)} %pad_maximum_fusion), channel_id=1, replica_groups=mesh['seq'=8,'exp'=32] {'seq'}, use_global_device_ids=true, to_apply=%region_9.0 | all-reduce | flops 53504 | bytes 321536 | tf_op jit(solution)/shard_map/psum | solution.py:109
  250.7 3.2 multiply_reduce_fusion.3
  253.9 51.0 %all-reduce.13.cloned.1.call-done = f32[32,1664]{1,0:T(8,128)} async-done(((f32[32,1664]{1,0:T(8,128)}), f32[32,1664]{1,0:T(8,128)}) %all-reduce.13.cloned.1.call-update) | async-done | bytes 213008 | tf_op jit(solution)/shard_map/psum | solution.py:109
  304.9 1.9 multiply_reduce_fusion.2
  307.3 132.5 %all-reduce.2 = (f32[1024]{0:T(1024)}, f32[1024]{0:T(1024)}, f32[1024]{0:T(1024)S(1)}) all-reduce(f32[1024]{0:T(1024)} %get-tuple-element.34, f32[1024]{0:T(1024)S(1)} %dynamic-update-slice.1, f32[1024]{0:T(1024)S(1)} %copy-done.14), channel_id=1, replica_groups=mesh['seq'=8,'exp'=32] {'exp'}, use_global_device_ids=true, to_apply=%region_11.0 | all-reduce | flops 3072 | bytes 24576 | tf_op jit(solution)/shard_map/psum | solution.py:105
  439.8 5.5 fusion.16
  447.2 0.8 dynamic-slice.3
  448.0 1.7 convolution_convert_fusion.1
  449.7 1.3 copy.57
  451.0 0.6 slice_bitcast_fusion
  451.6 1.8 convolution_convert_fusion
  453.5 1.3 dynamic_slice.22
  454.7 89.4 %all-reduce.15.cloned.1.call-done = f32[32,1664]{1,0:T(8,128)} async-done(((f32[32,1664]{1,0:T(8,128)}), f32[32,1664]{1,0:T(8,128)}) %all-reduce.15.cloned.1.call-update) | async-done | bytes 213008 | tf_op jit(solution)/shard_map/psum | solution.py:183
  544.1 1.1 multiply_reduce_fusion
  545.3 1.7 subtract_divide_fusion
  547.0 3.2 fusion.12
  550.2 22.4 %all-gather.8.cloned.1.call-done = bf16[1024,1664]{1,0:T(8,128)(2,1)} async-done(((bf16[32,1664]{1,0:T(8,128)(2,1)}), bf16[1024,1664]{1,0:T(8,128)(2,1)}) %all-gather.8.cloned.1.call-update) | async-done | bytes 3407888 | tf_op jit(solution)/shard_map/all_gather | solution.py:190
  572.6 3.7 fusion.10
  576.3 59.0 %all-gather.6.cloned.1.call-done = bf16[1024,1664]{1,0:T(8,128)(2,1)} async-done(((bf16[32,1664]{1,0:T(8,128)(2,1)}), bf16[1024,1664]{1,0:T(8,128)(2,1)}) %all-gather.6.cloned.1.call-update) | async-done | bytes 3407888 | tf_op jit(solution)/shard_map/all_gather | solution.py:189
  635.3 5.5 multiply_reduce_fusion.1
  640.8 3.5 convolution_add_fusion
  (59 shorter events, 2.9 us)
Async XLA Ops:
  8.0 87.1 %copy-start = (bf16[1024,1664]{1,0:T(8,128)(2,1)S(1)}, bf16[1024,1664]{1,0:T(8,128)(2,1)}, u32[]{:S(2)}) copy-start(bf16[1024,1664]{1,0:T(8,128)(2,1)} %param.8) | copy-start | bytes 10223620
  8.0 152.4 %all-reduce.11.cloned.1.call-start = ((), (), s32[]{:S(2)}) async-start(), calls=%async_computation.1 | async-start | bytes 425984 | tf_op jit(solution)/shard_map/psum | solution.py:109
  8.1 3.1 copy-start.1
  11.2 5.0 copy-start.13
  11.2 5.0 copy-start.5
  16.3 0.6 copy-start.16
  17.6 3.9 copy-start.2
  23.0 282.0 %all-reduce.13.cloned.1.call-start = ((), (), s32[]{:S(2)}) async-start(), calls=%async_computation.2 | async-start | bytes 425984 | tf_op jit(solution)/shard_map/psum | solution.py:109
  94.5 0.6 copy-start.10
  96.5 59.4 %copy-start.9 = (f32[2,4,4,4]{3,2,1,0:T(4,128)S(1)}, f32[2,4,4,4]{3,2,1,0:T(4,128)}, u32[]{:S(2)}) copy-start(f32[2,4,4,4]{3,2,1,0:T(4,128)} %param.10) | copy-start | bytes 1540
  148.5 2.9 copy-start.7
  150.2 1.2 copy-start.3
  165.2 7.6 %copy-start.15 = (f32[2,4,4,4]{3,2,1,0:T(4,128)S(1)}, f32[2,4,4,4]{3,2,1,0:T(4,128)}, u32[]{:S(2)}) copy-start(f32[2,4,4,4]{3,2,1,0:T(4,128)} %param.12) | copy-start | bytes 1540
  202.3 341.8 %all-reduce.15.cloned.1.call-start = ((), (), s32[]{:S(2)}) async-start(), calls=%async_computation.5 | async-start | bytes 425984 | tf_op jit(solution)/shard_map/psum | solution.py:183
  203.7 101.2 %copy-start.18 = (f32[32]{0:T(128)S(1)}, f32[32]{0:T(128)}, u32[]{:S(2)}) copy-start(f32[32]{0:T(128)} %get-tuple-element.26) | copy-start | bytes 388
  203.7 103.6 %copy-start.14 = (f32[1024]{0:T(1024)S(1)}, f32[1024]{0:T(1024)}, u32[]{:S(2)}) copy-start(f32[1024]{0:T(1024)} %dynamic-update-slice) | copy-start | bytes 12292
  203.7 236.1 %copy-start.11 = (f32[1024]{0:T(1024)S(1)}, f32[1024]{0:T(1024)}, u32[]{:S(2)}) copy-start(f32[1024]{0:T(1024)} %copy-done.10) | copy-start | bytes 12292
  306.8 0.5 copy-start.20
  445.3 101.7 %all-gather.4.cloned.1.call-start = ((), (), s32[]{:S(2)}) async-start(), calls=%async_computation | async-start | bytes 3514368 | tf_op jit(solution)/shard_map/all_gather | solution.py:191
  445.9 126.6 %all-gather.8.cloned.1.call-start = ((), (), s32[]{:S(2)}) async-start(), calls=%async_computation.4 | async-start | bytes 3514368 | tf_op jit(solution)/shard_map/all_gather | solution.py:190
  446.5 188.8 %all-gather.6.cloned.1.call-start = ((), (), s32[]{:S(2)}) async-start(), calls=%async_computation.3 | async-start | bytes 3514368 | tf_op jit(solution)/shard_map/all_gather | solution.py:189
  447.1 3.9 copy-start.12
  447.1 4.5 copy-start.4
  447.1 4.5 copy-start.8
  448.0 96.1 %copy-start.6 = (bf16[32,1664]{1,0:T(8,128)(2,1)S(1)}, bf16[32,1664]{1,0:T(8,128)(2,1)}, u32[]{:S(2)}) copy-start(bf16[32,1664]{1,0:T(8,128)(2,1)} %param.9) | copy-start | bytes 319492
  448.0 96.1 %copy-start.17 = (f32[32]{0:T(128)S(1)}, f32[32]{0:T(128)}, u32[]{:S(2)}) copy-start(f32[32]{0:T(128)} %copy-done.16) | copy-start | bytes 388
  547.0 88.3 %copy-start.19 = (f32[1024]{0:T(1024)S(1)}, f32[1024]{0:T(1024)}, u32[]{:S(2)}) copy-start(f32[1024]{0:T(1024)} %get-tuple-element.21) | copy-start | bytes 12292
Sparse Core Ops, SparseCore 0:
  23.1 102.7 all-reduce.10
  202.4 102.4 all-reduce.12
  445.5 98.6 all-reduce.14
Sparse Core Ops, SparseCore 1:
  447.7 62.2 all-gather.3
  511.8 60.7 all-gather.7
  574.3 61.0 all-gather.5
where the time goes:
time: 653 us; the launch traced here: 652 us
  blocking collectives  301 us (46%)
  waiting for transfers between devices  223 us (34%)
  matrix products  55.9 us (9%)
  local copies, waits for them, and re-layouts  38.1 us (6%)
  other arithmetic  16.5 us (3%)
  between operations  16.3 us (2%)
    psum x2, blocking collectives, token_total(): return lax.psum(partial_sums, 'exp')  204 us
    psum x2, blocking collectives, slot_total(): return lax.psum((first_part, second_part), 'seq')  97.3 us
    psum x1, waiting for transfers between devices, local(): lax.psum(jnp.dot(logit_grad_b, token_unit_b, preferred_element_type=jnp.f...  89.4 us
    all_gather x1, waiting for transfers between devices, local(): lax.all_gather(input_grad_b, 'exp', axis=0, tiled=True)  59 us
    psum x2, waiting for transfers between devices, slot_total(): return lax.psum((first_part, second_part), 'seq')  51 us
    all_gather x1, waiting for transfers between devices, local(): lax.all_gather(slot_out_b, 'exp', axis=0, tiled=True)  22.4 us
  transfers between devices with their start and end apart: 6, of which 4 were waited for; matrix products, arithmetic and copies ran while one was open for 5% of the time, Pallas kernels for 0%

commit v1 on v0

--- a/solution.py
+++ b/solution.py
@@ -1,3 +1,4 @@
+import functools
 import jax
 import jax.numpy as jnp
 from jax import lax
@@ -7,6 +8,14 @@
 norm_eps = 1e-06
 gelu_coef = 0.7978845608028654
 cubic_coef = 0.044715
+
+
+def _use_pages(view, net_axis):
+    current_block = lax.all_gather(view, axis_name=net_axis).sum(axis=0)
+    return current_block
+
+
+edit_tasks_here = functools.partial(_use_pages, net_axis="seq")
 
 
 def gelu_pair(preact):
@@ -180,8 +189,8 @@
         dispatch_grad - dispatch_dot[:, None]
     )
     logit_grad_b = (logit_gain * logit_grad).astype(jnp.bfloat16)
-    slot_unit_grad = lax.psum(
-        jnp.dot(logit_grad_b, token_unit_b, preferred_element_type=jnp.float32), "seq"
+    slot_unit_grad = edit_tasks_here(
+        jnp.dot(logit_grad_b, token_unit_b, preferred_element_type=jnp.float32)
     )
     grad_slots = unit_grad(slot_unit, slot_unit_grad, slot_norm)
     row_count = tokens.shape[0] // lax.axis_size("exp")

time: 653 us -> 717 us (1.098)
  waiting for transfers between devices: 223 us -> 287 us
    psum x1 -> x0, waiting for transfers between devices: 89.4 us -> none  [local(): lax.psum(jnp.dot(logit_grad_b, token_unit_b, preferred_element_type=jnp.f...]
    all_gather x0 -> x1, waiting for transfers between devices: none -> 59.4 us  [_use_pages(): current_block = lax.all_gather(view, axis_name=net_axis).sum(axis=0)]
    all_gather x1, waiting for transfers between devices: 0.01 us -> 56 us  [local(): lax.all_gather(slot_unit_b, 'exp', axis=0, tiled=True)]
    all_gather x1, waiting for transfers between devices: 22.4 us -> 59.5 us  [local(): lax.all_gather(slot_out_b, 'exp', axis=0, tiled=True)]
  transfers between devices with their start and end apart: 6 -> 6, of which waited for: 4 -> 5; matrix products, arithmetic and copies ran while one was open for 5% -> 5% of each run, Pallas kernels for 0% -> 0%
where the time goes in v1:
time: 717 us; the launch traced here: 715 us
  blocking collectives  300 us (42%)
  waiting for transfers between devices  287 us (40%)
  matrix products  55.9 us (8%)
  local copies, waits for them, and re-layouts  38.2 us (5%)
  other arithmetic  18.7 us (3%)
  between operations  14.9 us (2%)
    psum x2, blocking collectives, token_total(): return lax.psum(partial_sums, 'exp')  204 us
    psum x2, blocking collectives, slot_total(): return lax.psum((first_part, second_part), 'seq')  96.2 us
    all_gather x1, waiting for transfers between devices, local(): lax.all_gather(slot_out_b, 'exp', axis=0, tiled=True)  59.5 us
    all_gather x1, waiting for transfers between devices, _use_pages(): current_block = lax.all_gather(view, axis_name=net_axis).sum(axis=0)  59.4 us
    all_gather x1, waiting for transfers between devices, local(): lax.all_gather(input_grad_b, 'exp', axis=0, tiled=True)  58.9 us
    all_gather x1, waiting for transfers between devices, local(): lax.all_gather(slot_unit_b, 'exp', axis=0, tiled=True)  56 us
    psum x2, waiting for transfers between devices, slot_total(): return lax.psum((first_part, second_part), 'seq')  51.7 us
  transfers between devices with their start and end apart: 6, of which 5 were waited for; matrix products, arithmetic and copies ran while one was open for 5% of the time, Pallas kernels for 0%

profile of v1, /device:TPU:1, one launch (start us, length us, event | category | flops | bytes accessed | tf_op | source)
XLA Modules:
  0.0 715.2 jit_solution(1411290285244020100)
XLA Ops:
  7.2 2.9 fusion
  10.4 5.0 convert_divide_fusion
  16.1 0.7 fusion.55
  16.8 3.9 fusion.57
  20.7 1.4 fusion.39
  22.2 71.5 %psum.57 = f32[1024]{0:T(1024)S(1)} all-reduce(f32[1024]{0:T(1024)S(1)} %get-tuple-element.19), channel_id=1, replica_groups=mesh['seq'=8,'exp'=32] {'exp'}, use_global_device_ids=true, to_apply=%region_5.0 | all-reduce | flops 1024 | bytes 8192 | tf_op jit(solution)/shard_map/psum | solution.py:114
  94.3 1.4 fusion.41
  95.6 50.6 %all-reduce.13 = (bf16[32,1664]{1,0:T(8,128)(2,1)}, f32[32]{0:T(128)}) all-reduce(f32[32,1664]{1,0:T(8,128)} %fusion.41, f32[32]{0:T(128)} %get-tuple-element.18), channel_id=1, replica_groups=mesh['seq'=8,'exp'=32] {'seq'}, use_global_device_ids=true, to_apply=%region_6.0 | all-reduce | flops 53280 | bytes 319744 | tf_op jit(solution)/shard_map/psum | solution.py:118
  146.2 1.7 reshape_reshape.7
  148.0 1.7 copy.55
  149.7 1.2 copy-done.3
  150.9 1.1 fusion.66
  152.0 1.8 reshape.84
  153.9 1.4 copy.34
  155.3 0.7 copy.38
  156.0 1.3 dynamic-slice.4
  157.9 0.6 broadcast.43.clone.1
  158.5 1.4 dynamic-update-slice
  159.9 1.7 fusion.46
  161.6 1.7 reshape.108
  163.3 1.4 fusion.1
  164.7 1.1 copy.25
  165.8 2.3 reshape.85
  168.1 2.7 fusion.67
  170.7 1.6 reshape.87
  172.3 2.0 fusion.2
  174.3 1.9 convolution_bitcast_fusion.3
  176.2 2.0 fusion.15
  178.2 1.5 reshape.88
  179.7 2.9 fusion.68
  182.5 2.5 reshape.89
  185.1 2.2 convolution_bitcast_fusion.2
  187.3 0.8 copy.30
  188.1 1.4 copy.32
  189.6 1.8 copy.28
  191.3 1.8 reshape.91
  193.1 2.9 fusion.69
  196.0 1.8 reshape.92
  197.8 2.2 convolution_bitcast_fusion
  199.9 1.9 reshape.90
  201.9 1.3 pad_maximum_fusion
  203.2 45.6 %all-reduce.14 = (bf16[32,1664]{1,0:T(8,128)(2,1)}, f32[2,2,4,4,4]{4,3,2,1,0:T(4,128)}) all-reduce(f32[32,1664]{1,0:T(8,128)} %reshape.92, f32[2,2,4,4,4]{4,3,2,1,0:T(4,128)} %pad_maximum_fusion), channel_id=1, replica_groups=mesh['seq'=8,'exp'=32] {'seq'}, use_global_device_ids=true, to_apply=%region_9.0 | all-reduce | flops 53504 | bytes 321536 | tf_op jit(solution)/shard_map/psum | solution.py:118
  248.8 3.3 multiply_reduce_fusion.3
  252.1 51.7 %all-reduce.12.cloned.1.call-done = f32[32,1664]{1,0:T(8,128)} async-done(((f32[32,1664]{1,0:T(8,128)}), f32[32,1664]{1,0:T(8,128)}) %all-reduce.12.cloned.1.call-update) | async-done | bytes 213008 | tf_op jit(solution)/shard_map/psum | solution.py:118
  303.7 1.9 multiply_reduce_fusion.2
  306.2 132.5 %all-reduce.2 = (f32[1024]{0:T(1024)}, f32[1024]{0:T(1024)}, f32[1024]{0:T(1024)S(1)}) all-reduce(f32[1024]{0:T(1024)} %get-tuple-element.34, f32[1024]{0:T(1024)S(1)} %dynamic-update-slice.1, f32[1024]{0:T(1024)S(1)} %copy-done.14), channel_id=1, replica_groups=mesh['seq'=8,'exp'=32] {'exp'}, use_global_device_ids=true, to_apply=%region_11.0 | all-reduce | flops 3072 | bytes 24576 | tf_op jit(solution)/shard_map/psum | solution.py:114
  438.7 5.5 fusion.16
  446.0 0.8 dynamic-slice.3
  446.9 1.6 convolution_convert_fusion.1
  448.5 1.3 copy.57
  449.8 0.6 slice_bitcast_fusion
  450.4 1.8 convolution_convert_fusion
  452.3 1.3 dynamic_slice.22
  453.6 59.4 %all-gather.12.cloned.1.call-done = f32[256,1664]{1,0:T(8,128)} async-done(((f32[32,1664]{1,0:T(8,128)}), f32[256,1664]{1,0:T(8,128)}) %all-gather.12.cloned.1.call-update) | async-done | bytes 1703952 | tf_op jit(solution)/shard_map/all_gather | solution.py:14
  513.0 2.2 reduce_sum.88
  515.2 1.1 multiply_reduce_fusion
  516.4 1.7 subtract_divide_fusion
  518.1 56.0 %all-gather.6.cloned.1.call-done = bf16[1024,1664]{1,0:T(8,128)(2,1)} async-done(((bf16[32,1664]{1,0:T(8,128)(2,1)}), bf16[1024,1664]{1,0:T(8,128)(2,1)}) %all-gather.6.cloned.1.call-update) | async-done | bytes 3407888 | tf_op jit(solution)/shard_map/all_gather | solution.py:200
  574.1 3.1 fusion.12
  577.3 59.5 %all-gather.10.cloned.1.call-done = bf16[1024,1664]{1,0:T(8,128)(2,1)} async-done(((bf16[32,1664]{1,0:T(8,128)(2,1)}), bf16[1024,1664]{1,0:T(8,128)(2,1)}) %all-gather.10.cloned.1.call-update) | async-done | bytes 3407888 | tf_op jit(solution)/shard_map/all_gather | solution.py:199
  636.8 3.7 fusion.10
  640.5 58.9 %all-gather.8.cloned.1.call-done = bf16[1024,1664]{1,0:T(8,128)(2,1)} async-done(((bf16[32,1664]{1,0:T(8,128)(2,1)}), bf16[1024,1664]{1,0:T(8,128)(2,1)}) %all-gather.8.cloned.1.call-update) | async-done | bytes 3407888 | tf_op jit(solution)/shard_map/all_gather | solution.py:198
  699.4 5.5 multiply_reduce_fusion.1
  704.9 3.5 convolution_add_fusion
  (60 shorter events, 4.1 us)
Async XLA Ops:
  7.2 87.1 %copy-start = (bf16[1024,1664]{1,0:T(8,128)(2,1)S(1)}, bf16[1024,1664]{1,0:T(8,128)(2,1)}, u32[]{:S(2)}) copy-start(bf16[1024,1664]{1,0:T(8,128)(2,1)} %param.8) | copy-start | bytes 10223620
  7.2 152.7 %all-reduce.10.cloned.1.call-start = ((), (), s32[]{:S(2)}) async-start(), calls=%async_computation.1 | async-start | bytes 425984 | tf_op jit(solution)/shard_map/psum | solution.py:118
  7.2 3.1 copy-start.1
  10.4 5.0 copy-start.13
  10.4 5.0 copy-start.5
  15.5 0.6 copy-start.16
  16.8 3.9 copy-start.2
  22.1 281.6 %all-reduce.12.cloned.1.call-start = ((), (), s32[]{:S(2)}) async-start(), calls=%async_computation.2 | async-start | bytes 425984 | tf_op jit(solution)/shard_map/psum | solution.py:118
  93.7 0.6 copy-start.10
  95.6 59.7 %copy-start.9 = (f32[2,4,4,4]{3,2,1,0:T(4,128)S(1)}, f32[2,4,4,4]{3,2,1,0:T(4,128)}, u32[]{:S(2)}) copy-start(f32[2,4,4,4]{3,2,1,0:T(4,128)} %param.10) | copy-start | bytes 1540
  148.0 2.9 copy-start.7
  149.7 1.2 copy-start.3
  164.7 7.6 %copy-start.15 = (f32[2,4,4,4]{3,2,1,0:T(4,128)S(1)}, f32[2,4,4,4]{3,2,1,0:T(4,128)}, u32[]{:S(2)}) copy-start(f32[2,4,4,4]{3,2,1,0:T(4,128)} %param.12) | copy-start | bytes 1540
  201.8 311.1 %all-gather.12.cloned.1.call-start = ((), (), s32[]{:S(2)}) async-start(), calls=%async_computation.5 | async-start | bytes 1916928 | tf_op jit(solution)/shard_map/all_gather | solution.py:14
  203.2 100.5 %copy-start.18 = (f32[32]{0:T(128)S(1)}, f32[32]{0:T(128)}, u32[]{:S(2)}) copy-start(f32[32]{0:T(128)} %get-tuple-element.26) | copy-start | bytes 388
  203.2 102.9 %copy-start.14 = (f32[1024]{0:T(1024)S(1)}, f32[1024]{0:T(1024)}, u32[]{:S(2)}) copy-start(f32[1024]{0:T(1024)} %dynamic-update-slice) | copy-start | bytes 12292
  203.2 235.4 %copy-start.11 = (f32[1024]{0:T(1024)S(1)}, f32[1024]{0:T(1024)}, u32[]{:S(2)}) copy-start(f32[1024]{0:T(1024)} %copy-done.10) | copy-start | bytes 12292
  305.7 0.5 copy-start.20
  444.2 130.0 %all-gather.6.cloned.1.call-start = ((), (), s32[]{:S(2)}) async-start(), calls=%async_computation | async-start | bytes 3514368 | tf_op jit(solution)/shard_map/all_gather | solution.py:200
  444.8 192.0 %all-gather.10.cloned.1.call-start = ((), (), s32[]{:S(2)}) async-start(), calls=%async_computation.4 | async-start | bytes 3514368 | tf_op jit(solution)/shard_map/all_gather | solution.py:199
  445.3 254.1 %all-gather.8.cloned.1.call-start = ((), (), s32[]{:S(2)}) async-start(), calls=%async_computation.3 | async-start | bytes 3514368 | tf_op jit(solution)/shard_map/all_gather | solution.py:198
  445.9 3.9 copy-start.12
  445.9 4.5 copy-start.4
  445.9 4.5 copy-start.8
  448.5 66.7 %copy-start.6 = (bf16[32,1664]{1,0:T(8,128)(2,1)S(1)}, bf16[32,1664]{1,0:T(8,128)(2,1)}, u32[]{:S(2)}) copy-start(bf16[32,1664]{1,0:T(8,128)(2,1)} %param.9) | copy-start | bytes 319492
  448.5 66.7 %copy-start.17 = (f32[32]{0:T(128)S(1)}, f32[32]{0:T(128)}, u32[]{:S(2)}) copy-start(f32[32]{0:T(128)} %copy-done.16) | copy-start | bytes 388
  518.1 181.3 %copy-start.19 = (f32[1024]{0:T(1024)S(1)}, f32[1024]{0:T(1024)}, u32[]{:S(2)}) copy-start(f32[1024]{0:T(1024)} %get-tuple-element.21) | copy-start | bytes 12292
Sparse Core Ops, SparseCore 0:
  22.3 102.7 all-reduce.9
  202.0 101.7 all-reduce.11
  444.3 68.6 all-gather.11
  514.7 59.3 all-gather.5
  575.8 60.9 all-gather.9
  638.5 60.8 all-gather.7
